TPU v7x, 32 devices: a whole 2x2x4 slice. The times are simulated.
32 devices in a mesh: gx: 16 (over z, y, x), gy: 2 (over core).
Axes of the slice: x: 2, y: 2, z: 4, core: 2. Of those that a mesh axis runs over, the one named last changes fastest.
Arguments:
- density: float32 [128, 32, 64], P('gx', None, 'gy'), may hold values from 0.5 to 1.5
- momentum: float32 [3, 128, 32, 64], P(None, 'gx', None, 'gy'), may hold values from -3 to 3
- energy: float32 [128, 32, 64], P('gx', None, 'gy'), may hold values from 2.5 to 4
- eddy_normal_cell: int32 [1024], P('gx'), may hold values from 0 to 63
- eddy_spanwise_cell: int32 [1024], P('gx'), may hold values from 0 to 31
- eddy_signs: int32 [1024, 3], P('gx'), may hold values from 0 to 1
- eddy_strengths: float32 [1024], P('gx'), may hold values from 0.3 to 3
- filter_matrices: float32 [1, 128, 128], replicated, may hold values from -1.25 to 1.25
- shock_switch: int32 [1, 64], P(None, 'gy'), may hold values 0 or 1
- dilatation_bin: int32 [128, 32, 64], P('gx', None, 'gy'), may hold values from 0 to 63
- vorticity_bin: int32 [128, 32, 64], P('gx', None, 'gy'), may hold values from 0 to 63, as said below
Outputs:
- conserved_next: float32 [5, 128, 32, 64], P(None, 'gx', None, 'gy')
- histogram: float32 [64, 64], replicated
Inputs may be any that keep to these rules, and one draw needn't show every extreme that they name: vorticity_bin at streamwise cell x is x * 64 // 128 or one more, modulo 64.
All inputs are finite; a program needn't handle non-finite values. No bound on the sum of `shock_switch` on one device may be relied on, other than what follows from the above.
Results may differ from a plain program's by a relative error of at most 0.0003.
Values sent between devices are 32-bit elements; how exact they have to be, the bound alone decides.
No kernel may reach another device: no remote copies, remote signals or barrier semaphores. Data moves between devices by JAX's collectives and lax.ppermute only.
A program may use at most 64 MiB of HBM per device.

v0:
```python
import math
import jax
import jax.numpy as jnp
from jax import lax
from jax.sharding import PartitionSpec as P

HISTOGRAM_BINS = 64
SIGMA_Y = 32
SIGMA_Z = 8
TIME_STEP = 0.1
GAMMA_GAS = 1.4
SENSOR_EPS = 0.1
HAT_PEAK = math.sqrt(1.5)


def extended(x, sides, width):
    for axis, dim in sides:
        size, length = (lax.axis_size(axis), x.shape[dim])
        up = [(i, (i + 1) % size) for i in range(size - 1)]
        down = [(j, i) for i, j in up]
        last = lax.slice_in_dim(x, length - width, length, axis=dim)
        first = lax.slice_in_dim(x, 0, width, axis=dim)
        before = lax.ppermute(last, axis, up)
        after = lax.ppermute(first, axis, down)
        x = jnp.concatenate([before, x, after], axis=dim)
    return x


def hat_shape(centres, coords, spread, period):
    offset = coords[None, :] - centres[:, None]
    if period > 0:
        offset = jnp.mod(offset + period / 2, period) - period / 2
    return HAT_PEAK * jnp.maximum(0.0, 1.0 - jnp.abs(offset) / spread)


def inflow_from(centre_y, centre_z, eddy_weight, coords_y, coords_z, span):
    shape_y = hat_shape(centre_y, coords_y, float(SIGMA_Y), 0)
    shape_z = hat_shape(centre_z, coords_z, float(SIGMA_Z), span)
    weighted = (eddy_weight[:, :, None] * shape_z[:, None, :]).reshape(eddy_weight.shape[0], -1)
    inflow = jnp.dot(weighted.T, shape_y, precision=lax.Precision.HIGHEST)
    return inflow.reshape(3, coords_z.shape[0], coords_y.shape[0])


def ghost_state(inflow):
    mom_x = 1.0 + inflow[0]
    kinetic = mom_x * mom_x + inflow[1] * inflow[1] + inflow[2] * inflow[2]
    return jnp.stack([jnp.ones_like(mom_x), mom_x, inflow[1], inflow[2], 3.0 + 0.5 * kinetic])


def flux_of(fields, velocity, pressure, direction):
    result = fields * velocity[direction][None]
    result = result.at[1 + direction].add(pressure)
    return result.at[4].add(pressure * velocity[direction])


def central_x(values):
    return (values[..., 2:, :, 1:-1] - values[..., :-2, :, 1:-1]) * 0.5


def central_y(values):
    return (values[..., 1:-1, :, 2:] - values[..., 1:-1, :, :-2]) * 0.5


def central_z(values):
    centre = values[..., 1:-1, :, 1:-1]
    return (jnp.roll(centre, -1, axis=-2) - jnp.roll(centre, 1, axis=-2)) * 0.5


def section_rhs(padded):
    velocity = padded[1:4] / padded[0][None]
    pressure = (GAMMA_GAS - 1.0) * (padded[4] - 0.5 * jnp.sum(padded[1:4] * velocity, axis=0))
    change = central_x(flux_of(padded, velocity, pressure, 0))
    change = change + central_y(flux_of(padded, velocity, pressure, 1))
    change = change + central_z(flux_of(padded, velocity, pressure, 2))
    updated = padded[:, 1:-1, :, 1:-1] - TIME_STEP * change
    dilatation = central_x(velocity[0]) + central_y(velocity[1]) + central_z(velocity[2])
    vort_x = central_y(velocity[2]) - central_z(velocity[1])
    vort_y = central_z(velocity[0]) - central_x(velocity[2])
    vort_z = central_x(velocity[1]) - central_y(velocity[0])
    squared = dilatation * dilatation
    shock_sensor = squared / (
        squared + vort_x * vort_x + vort_y * vort_y + vort_z * vort_z + SENSOR_EPS
    )
    return (updated, shock_sensor)


def filter_lines(pencil, filter_matrices):
    block_count, block_len = (filter_matrices.shape[0], filter_matrices.shape[1])
    lanes = pencil.shape[2]
    blocks = pencil.reshape(5, block_count, block_len, lanes)
    smooth = jnp.einsum("bij,fbjp->fbip", filter_matrices, blocks, precision=lax.Precision.HIGHEST)
    return smooth.reshape(5, block_count * block_len, lanes)


def plane_histogram(shock_sensor, dilatation_bin, vorticity_bin):
    bin_levels = jnp.arange(HISTOGRAM_BINS, dtype=jnp.int32)

    def accumulate_plane(histogram_totals, histogram_parts):
        sensor_plane, plane_dilatation, plane_vorticity = histogram_parts
        flat_sensor = sensor_plane.reshape(-1)
        dilatation_table = (plane_dilatation.reshape(-1)[None, :] == bin_levels[:, None]).astype(
            jnp.float32
        )
        vorticity_table = jnp.where(
            plane_vorticity.reshape(-1)[:, None] == bin_levels[None, :], flat_sensor[:, None], 0.0
        )
        return (
            histogram_totals
            + jnp.dot(dilatation_table, vorticity_table, precision=lax.Precision.HIGHEST),
            None,
        )

    histogram_totals, _ = lax.scan(
        accumulate_plane,
        jnp.zeros((HISTOGRAM_BINS, HISTOGRAM_BINS), jnp.float32),
        (shock_sensor, dilatation_bin, vorticity_bin),
    )
    return histogram_totals


def shards(
    density,
    momentum,
    energy,
    eddy_normal_cell,
    eddy_spanwise_cell,
    eddy_signs,
    eddy_strengths,
    filter_matrices,
    shock_switch,
    dilatation_bin,
    vorticity_bin,
):
    cells_x, span, cells_y = density.shape
    slab_index = lax.axis_index("gx")
    block_index = lax.axis_index("gy")
    slab_count = lax.axis_size("gx")
    fields = jnp.concatenate([density[None], momentum, energy[None]], axis=0)
    total_y = cells_y * lax.axis_size("gy")
    total_eddies = eddy_normal_cell.shape[0] * slab_count
    amplitude = math.sqrt(total_y * span / (total_eddies * SIGMA_Y * SIGMA_Z))
    eddy_weight = (2 * eddy_signs - 1).astype(jnp.float32) * eddy_strengths[:, None] * amplitude
    coords_y = (block_index * cells_y + jnp.arange(cells_y, dtype=jnp.int32)).astype(jnp.float32)
    coords_z = jnp.arange(span, dtype=jnp.int32).astype(jnp.float32)
    partial_sum = inflow_from(
        eddy_normal_cell.astype(jnp.float32),
        eddy_spanwise_cell.astype(jnp.float32),
        eddy_weight,
        coords_y,
        coords_z,
        span,
    )
    inflow = lax.psum(partial_sum, "gx")
    ghost_cells = ghost_state(inflow)
    padded = extended(fields, (("gx", 1), ("gy", 3)), 1)
    padded = padded.at[:, 0, :, 1:-1].set(
        jnp.where(slab_index == 0, ghost_cells, padded[:, 0, :, 1:-1])
    )
    padded = padded.at[:, -1, :, 1:-1].set(
        jnp.where(slab_index == slab_count - 1, fields[:, -1], padded[:, -1, :, 1:-1])
    )
    padded = padded.at[:, 1:-1, :, 0].set(
        jnp.where(block_index == 0, fields[:, :, :, 0], padded[:, 1:-1, :, 0])
    )
    padded = padded.at[:, 1:-1, :, -1].set(
        jnp.where(
            block_index == lax.axis_size("gy") - 1, fields[:, :, :, -1], padded[:, 1:-1, :, -1]
        )
    )
    updated, shock_sensor = section_rhs(padded)
    block_len = filter_matrices.shape[1]
    filter_row = slab_index * cells_x // block_len
    mask_row = lax.dynamic_slice_in_dim(shock_switch, filter_row, 1, 0).astype(jnp.float32)
    weight = mask_row[None] * shock_sensor
    columns = span * cells_y
    stacked = updated.reshape(5, cells_x, columns)
    weight_flat = weight.reshape(1, cells_x, columns)
    pencil, pencil_weight = (
        lax.all_to_all(stacked, "gx", split_axis=2, concat_axis=1, tiled=True),
        lax.all_to_all(weight_flat, "gx", split_axis=2, concat_axis=1, tiled=True),
    )
    smooth = filter_lines(pencil, filter_matrices)
    returned = pencil + pencil_weight * (smooth - pencil)
    back_lines = lax.all_to_all(returned, "gx", split_axis=1, concat_axis=2, tiled=True)
    conserved_next = back_lines.reshape(5, cells_x, span, cells_y)
    partial_histogram = plane_histogram(shock_sensor, dilatation_bin, vorticity_bin)
    summed = lax.psum(partial_histogram, ("gx", "gy"))
    all_cells = cells_x * slab_count * span * total_y
    histogram = summed * (HISTOGRAM_BINS * HISTOGRAM_BINS / all_cells)
    return (conserved_next, histogram)


def solution(mesh):
    in_specs = (
        P("gx", None, "gy"),
        P(None, "gx", None, "gy"),
        P("gx", None, "gy"),
        P("gx"),
        P("gx"),
        P("gx", None),
        P("gx"),
        P(),
        P(None, "gy"),
        P("gx", None, "gy"),
        P("gx", None, "gy"),
    )
    out_specs = (P(None, "gx", None, "gy"), P())
    return jax.shard_map(shards, mesh=mesh, in_specs=in_specs, out_specs=out_specs, check_vma=False)
```

profile of v0, /device:TPU:0, one launch (start us, length us, event | category | flops | bytes accessed | tf_op | source)
XLA Modules:
  0.0 215.9 jit_solution(9551707045615207745)
XLA Ops:
  0.6 0.9 pad_maximum_fusion.4
  1.6 1.3 collective-permute-start.1
  2.9 5.5 %collective-permute-start = (f32[5,1,32,32]{3,2,0,1:T(8,128)S(1)}, f32[5,1,32,32]{3,2,0,1:T(8,128)S(1)}, u32[]{:S(2)}, u32[]{:S(2)}) collective-permute-start(f32[5,1,32,32]{3,2,0,1:T(8,128)S(1)} %get-tuple-element.222), channel_id=1, source_target_pairs={{0,2},{2,4},{4,6},{6,8},{8,10},{10,12},{12,14},{14,16},{16,18},{18... | collective-permute-start | bytes 61448 | tf_op jit(solution)/shard_map/ppermute | solution.py:23
  10.8 75.6 %psum.14 = f32[3,32,32]{2,1,0:T(8,128)S(1)} all-reduce(f32[3,32,32]{2,1,0:T(8,128)S(1)} %fusion.50), channel_id=1, replica_groups=mesh['gx'=16,'gy'=2] {'gx'}, use_global_device_ids=true, to_apply=%region_1.2 | all-reduce | flops 3072 | bytes 24576 | tf_op jit(solution)/shard_map/psum | solution.py:153
  86.4 1.2 pad_maximum_fusion.2
  88.9 1.2 pad_maximum_fusion
  91.2 1.3 collective-permute-start.3
  92.5 3.0 %collective-permute-start.2 = (f32[5,10,32,1]{2,3,1,0:T(1,128)S(1)}, f32[5,10,32,1]{2,3,1,0:T(1,128)S(1)}, u32[]{:S(2)}, u32[]{:S(2)}) collective-permute-start(f32[5,10,32,1]{2,3,1,0:T(1,128)S(1)} %copy.81), channel_id=1, source_target_pairs={{0,1},{2,3},{4,5},{6,7},{8,9},{10,11},{12,13},{14,15},{16,17},{18,... | collective-permute-start | bytes 19208 | tf_op jit(solution)/shard_map/ppermute | solution.py:23
  95.5 1.4 and_reduce_fusion
  97.3 1.3 copy.84
  98.6 1.6 pad_maximum_fusion.1
  100.2 1.4 fusion.48
  101.6 1.7 scatter.14
  103.4 1.0 scatter.15
  105.9 3.7 %scatter.19 = f32[5,10,32,34]{3,2,0,1:T(8,128)S(1)} dynamic-update-slice(f32[5,10,32,34]{3,2,0,1:T(8,128)S(1)} %scatter.16, f32[5,8,32,1]{3,2,0,1:T(8,128)S(1)} %slice_select_fusion, s32[]{:T(128)} %constant.328.clone.1, s32[]{:T(128)} %constant.350.clone.1, s32[]{:T(128)} %constant.328.clone.1, s32[]{:T(128)} %constant.351.clone.1) | dynamic-update-slice | bytes 10244 | tf_op jit(solution)/shard_map/scatter | solution.py:165
  111.2 1.2 fusion.91
  112.8 1.0 copy.119
  114.4 3.7 %reduce.27 = f32[1024,8]{1,0:T(8,128)} reduce(f32[1024,1,8]{2,1,0:T(1,128)} %bitcast.128, f32[]{:T(128)} %broadcast.273), dimensions={1}, to_apply=%bitcast.110.reduce_sub_computation | reduce | bytes 65540
  118.1 1.9 reshape.467
  120.0 3.5 %all-to-all-start.1 = ((f32[16,1,512]{2,1,0:T(1,128)}), f32[16,1,512]{2,1,0:T(1,128)S(1)}, u32[]{:S(2)}, u32[]{:S(2)}) async-start(f32[16,1,512]{2,1,0:T(1,128)} %reshape.467), calls=%async_computation.1 | async-start | bytes 65536 | tf_op jit(solution)/shard_map/all_to_all | solution.py:180
  123.5 2.7 %fusion.14 = f32[5,8,32,32]{3,2,0,1:T(8,128)} fusion(f32[5,10,32,34]{3,2,0,1:T(8,128)S(1)} %get-tuple-element.221, f32[5,10,32,34]{3,2,0,1:T(8,128)S(1)} %scatter.19, f32[5,8,1,32]{3,2,0,1:T(1,128)S(1)} %get-tuple-element.213, f32[5,8,31,32]{3,2,0,1:T(8,128)} %get-tuple-element.215, f32[5,8,31,32]{3,2,0,1:T(8,128)S(1)} %get-tuple-element.214, ...), kind=kLoop, calls=%fused_computation.23 | loop fusion | flops 368640 | bytes 4295680 | tf_op jit(solution)/shard_map/sub | solution.py:75
  126.2 3.6 %copy.122 = f32[5,8,32,32]{1,0,3,2:T(8,128)} copy(f32[5,8,32,32]{3,2,0,1:T(8,128)} %fusion.14) | data formatting | bytes 327680 | tf_op jit(solution)/shard_map/reshape | solution.py:176
  129.8 3.4 %reshape.465 = f32[16,1,2560]{2,1,0:T(1,128)} reshape(f32[1024,5,8]{2,1,0:T(8,128)} %bitcast.117) | data formatting | bytes 327680
  133.1 6.9 %all-to-all-start = ((f32[16,1,2560]{2,1,0:T(1,128)}), f32[16,1,2560]{2,1,0:T(1,128)S(1)}, u32[]{:S(2)}, u32[]{:S(2)}) async-start(f32[16,1,2560]{2,1,0:T(1,128)} %reshape.465), calls=%async_computation | async-start | bytes 327680 | tf_op jit(solution)/shard_map/all_to_all | solution.py:179
  141.8 6.1 %all-to-all-done = f32[16,1,2560]{2,1,0:T(1,128)S(1)} async-done(((f32[16,1,2560]{2,1,0:T(1,128)}), f32[16,1,2560]{2,1,0:T(1,128)S(1)}, u32[]{:S(2)}, u32[]{:S(2)}) %all-to-all-start) | async-done | bytes 163872 | tf_op jit(solution)/shard_map/all_to_all | solution.py:179
  148.9 2.6 %reshape.466 = f32[1024,5,8]{2,1,0:T(8,128)} reshape(f32[16,2560]{1,0:T(8,128)S(1)} %reduce.26) | data formatting | bytes 327680
  151.5 2.6 %copy.103 = f32[5,16,8,64]{3,2,1,0:T(8,128)S(1)} copy(f32[5,16,8,64]{2,0,3,1:T(8,128)} %bitcast.118) | data formatting | bytes 327680 | tf_op jit(solution)/shard_map/all_to_all | solution.py:179
  156.1 3.5 %all-to-all-start.2 = ((f32[16,1,2560]{2,1,0:T(1,128)}), f32[16,1,2560]{2,1,0:T(1,128)S(1)}, u32[]{:S(2)}, u32[]{:S(2)}) async-start(f32[16,1,2560]{2,1,0:T(1,128)} %reshape.469), calls=%async_computation.2 | async-start | bytes 327680 | tf_op jit(solution)/shard_map/all_to_all | solution.py:184
  159.6 12.6 %while.22 = (s32[]{:T(128)}, f32[64,64]{1,0:T(8,128)S(1)}, s32[8,32,32]{2,1,0:T(8,128)}, s32[8,32,32]{2,1,0:T(8,128)}, f32[8,32,32]{2,1,0:T(8,128)S(1)}, /*index=5*/s32[]{:T(128)}, s32[]{:T(128)}) while((s32[]{:T(128)}, f32[64,64]{1,0:T(8,128)S(1)}, s32[8,32,32]{2,1,0:T(8,128)}, s32[8,32,32]{2,1,0:T(8,128)}, ...), condition=%wide.region_4.5_spmd.clone.clone, body=%wide.region_3.4_spmd.clone.clone.sunk | while | flops 50536448 | bytes 94311 | solution.py:113
  172.2 40.8 %psum.15 = f32[64,64]{1,0:T(8,128)S(1)} all-reduce(f32[64,64]{1,0:T(8,128)S(1)} %get-tuple-element.157), channel_id=1, replica_groups=mesh['gx'=16,'gy'=2] {'gx','gy'}, use_global_device_ids=true, to_apply=%region_5.6 | all-reduce | flops 4096 | bytes 32768 | tf_op jit(solution)/shard_map/psum | solution.py:187
  213.6 0.9 reduce.29
  214.9 1.0 reshape.460
  (117 shorter events, 27.0 us)
Async XLA Ops:
  0.6 153.6 %copy-start = (f32[1,128,128]{2,1,0:T(8,128)S(1)}, f32[1,128,128]{2,1,0:T(8,128)}, u32[]{:S(2)}) copy-start(f32[1,128,128]{2,1,0:T(8,128)} %param.40) | copy-start | bytes 196612
  1.6 93.9 %copy-start.4 = (s32[4]{0:T(128)S(1)}, s32[4]{0:T(128)}, u32[]{:S(2)}) copy-start(s32[4]{0:T(128)} %constant.330.clone.1) | copy-start | bytes 52
  1.6 87.3 %collective-permute-start.1 = (f32[5,1,32,32]{3,2,0,1:T(8,128)S(1)}, f32[5,1,32,32]{3,2,0,1:T(8,128)S(1)}, u32[]{:S(2)}, u32[]{:S(2)}) collective-permute-start(f32[5,1,32,32]{3,2,0,1:T(8,128)S(1)} %get-tuple-element.223), channel_id=1, source_target_pairs={{2,0},{4,2},{6,4},{8,6},{10,8},{12,10},{14,12},{16,14},{18,16},{20... | collective-permute-start | bytes 61448 | tf_op jit(solution)/shard_map/ppermute | solution.py:24
  2.9 86.0 %collective-permute-start = (f32[5,1,32,32]{3,2,0,1:T(8,128)S(1)}, f32[5,1,32,32]{3,2,0,1:T(8,128)S(1)}, u32[]{:S(2)}, u32[]{:S(2)}) collective-permute-start(f32[5,1,32,32]{3,2,0,1:T(8,128)S(1)} %get-tuple-element.222), channel_id=1, source_target_pairs={{0,2},{2,4},{4,6},{6,8},{8,10},{10,12},{12,14},{14,16},{16,18},{18... | collective-permute-start | bytes 61448 | tf_op jit(solution)/shard_map/ppermute | solution.py:23
  87.6 11.0 %copy-start.1 = (f32[3,8,32,32]{3,2,1,0:T(8,128)S(1)}, f32[3,8,32,32]{3,2,1,0:T(8,128)}, u32[]{:S(2)}) copy-start(f32[3,8,32,32]{3,2,1,0:T(8,128)} %param.34) | copy-start | bytes 294916
  87.6 11.0 %copy-start.2 = (f32[8,32,32]{2,1,0:T(8,128)S(1)}, f32[8,32,32]{2,1,0:T(8,128)}, u32[]{:S(2)}) copy-start(f32[8,32,32]{2,1,0:T(8,128)} %param.35) | copy-start | bytes 98308
  87.6 11.0 %copy-start.3 = (f32[8,32,32]{2,1,0:T(8,128)S(1)}, f32[8,32,32]{2,1,0:T(8,128)}, u32[]{:S(2)}) copy-start(f32[8,32,32]{2,1,0:T(8,128)} %param.33) | copy-start | bytes 98308
  91.2 6.1 %collective-permute-start.3 = (f32[5,10,32,1]{2,3,1,0:T(1,128)S(1)}, f32[5,10,32,1]{2,3,1,0:T(1,128)S(1)}, u32[]{:S(2)}, u32[]{:S(2)}) collective-permute-start(f32[5,10,32,1]{2,3,1,0:T(1,128)S(1)} %copy.82), channel_id=1, source_target_pairs={{1,0},{3,2},{5,4},{7,6},{9,8},{11,10},{13,12},{15,14},{17,16},{19,... | collective-permute-start | bytes 19208 | tf_op jit(solution)/shard_map/ppermute | solution.py:24
  92.5 4.4 %collective-permute-start.2 = (f32[5,10,32,1]{2,3,1,0:T(1,128)S(1)}, f32[5,10,32,1]{2,3,1,0:T(1,128)S(1)}, u32[]{:S(2)}, u32[]{:S(2)}) collective-permute-start(f32[5,10,32,1]{2,3,1,0:T(1,128)S(1)} %copy.81), channel_id=1, source_target_pairs={{0,1},{2,3},{4,5},{6,7},{8,9},{10,11},{12,13},{14,15},{16,17},{18,... | collective-permute-start | bytes 19208 | tf_op jit(solution)/shard_map/ppermute | solution.py:23
  120.0 13.2 %all-to-all-start.1 = ((f32[16,1,512]{2,1,0:T(1,128)}), f32[16,1,512]{2,1,0:T(1,128)S(1)}, u32[]{:S(2)}, u32[]{:S(2)}) async-start(f32[16,1,512]{2,1,0:T(1,128)} %reshape.467), calls=%async_computation.1 | async-start | bytes 65536 | tf_op jit(solution)/shard_map/all_to_all | solution.py:180
  133.1 14.8 %all-to-all-start = ((f32[16,1,2560]{2,1,0:T(1,128)}), f32[16,1,2560]{2,1,0:T(1,128)S(1)}, u32[]{:S(2)}, u32[]{:S(2)}) async-start(f32[16,1,2560]{2,1,0:T(1,128)} %reshape.465), calls=%async_computation | async-start | bytes 327680 | tf_op jit(solution)/shard_map/all_to_all | solution.py:179
  156.1 57.5 %all-to-all-start.2 = ((f32[16,1,2560]{2,1,0:T(1,128)}), f32[16,1,2560]{2,1,0:T(1,128)S(1)}, u32[]{:S(2)}, u32[]{:S(2)}) async-start(f32[16,1,2560]{2,1,0:T(1,128)} %reshape.469), calls=%async_computation.2 | async-start | bytes 327680 | tf_op jit(solution)/shard_map/all_to_all | solution.py:184
where the time goes:
time: 218 us; the launch traced here: 216 us
  blocking collectives  116 us (53%)
  local copies, waits for them, and re-layouts  39.7 us (18%)
  starting transfers between devices  25 us (11%)
  other arithmetic  21.8 us (10%)
  waiting for transfers between devices  6.13 us (3%)
  matrix products  5.55 us (3%)
    psum x1, blocking collectives, shards(): inflow = lax.psum(partial_sum, 'gx')  75.6 us
    psum x1, blocking collectives, shards(): summed = lax.psum(partial_histogram, ('gx', 'gy'))  40.8 us
    unnamed x16, local copies, waits for them, and re-layouts  9.82 us
    ppermute x2, starting transfers between devices, extended(): before = lax.ppermute(last, axis, up)  8.5 us
    all_to_all x1, starting transfers between devices, shards(): lax.all_to_all(stacked, 'gx', split_axis=2, concat_axis=1, tiled=True)  6.88 us
    all_to_all x1, waiting for transfers between devices, shards(): lax.all_to_all(stacked, 'gx', split_axis=2, concat_axis=1, tiled=True)  6.11 us
    dynamic_slice x16, local copies, waits for them, and re-layouts, plane_histogram(): lax.scan(accumulate_plane, jnp.zeros((HISTOGRAM_BINS, HISTOGRAM_BINS), jn...  6 us
    dot_general x8, matrix products, accumulate_plane(): jnp.dot(dilatation_table, vorticity_table, precision=lax.Precision.HIGHEST)  4.61 us
  transfers between devices with their start and end apart: 7, of which 1 were waited for; matrix products, arithmetic and copies ran while one was open for 14% of the time, Pallas kernels for 0%

commit v1 on v0

--- a/solution.py
+++ b/solution.py
@@ -11,6 +11,13 @@
 GAMMA_GAS = 1.4
 SENSOR_EPS = 0.1
 HAT_PEAK = math.sqrt(1.5)
+
+
+def trade_parts(x, axis, split, join):
+    size = lax.axis_size(axis)
+    tiles = jnp.stack(jnp.split(x, size, axis=split), axis=0)
+    tiles = lax.all_to_all(tiles, axis, split_axis=0, concat_axis=0)
+    return jnp.concatenate(tiles, axis=join)
 
 
 def extended(x, sides, width):
@@ -176,7 +183,7 @@
     stacked = updated.reshape(5, cells_x, columns)
     weight_flat = weight.reshape(1, cells_x, columns)
     pencil, pencil_weight = (
-        lax.all_to_all(stacked, "gx", split_axis=2, concat_axis=1, tiled=True),
+        trade_parts(stacked, "gx", 2, 1),
         lax.all_to_all(weight_flat, "gx", split_axis=2, concat_axis=1, tiled=True),
     )
     smooth = filter_lines(pencil, filter_matrices)

time: 218 us -> 207 us (0.950)
  local copies, waits for them, and re-layouts: 39.7 us -> 32.8 us
  other arithmetic: 21.8 us -> 17.2 us
    all_to_all x3 -> x1, local copies, waits for them, and re-layouts: 3.26 us -> 0.54 us  [trade_parts(): tiles = lax.all_to_all(tiles, axis, split_axis=0, concat_axis=0)]
    unnamed x16 -> x41, local copies, waits for them, and re-layouts: 9.82 us -> 7.49 us
    reshape x1, local copies, waits for them, and re-layouts: 3.59 us -> 1.4 us  [shards(): stacked = updated.reshape(5, cells_x, columns)]
  transfers between devices with their start and end apart: 7 -> 7, of which waited for: 1 -> 2; matrix products, arithmetic and copies ran while one was open for 14% -> 11% of each run, Pallas kernels for 0% -> 0%
where the time goes in v1:
time: 207 us; the launch traced here: 205 us
  blocking collectives  116 us (56%)
  local copies, waits for them, and re-layouts  32.8 us (16%)
  starting transfers between devices  22.9 us (11%)
  other arithmetic  17.2 us (8%)
  waiting for transfers between devices  8.1 us (4%)
  matrix products  5.55 us (3%)
    psum x1, blocking collectives, shards(): inflow = lax.psum(partial_sum, 'gx')  75.7 us
    psum x1, blocking collectives, shards(): summed = lax.psum(partial_histogram, ('gx', 'gy'))  40.8 us
    ppermute x2, starting transfers between devices, extended(): before = lax.ppermute(last, axis, up)  8.5 us
    unnamed x41, local copies, waits for them, and re-layouts  7.49 us
    all_to_all x1, waiting for transfers between devices, trade_parts(): tiles = lax.all_to_all(tiles, axis, split_axis=0, concat_axis=0)  6.04 us
    dynamic_slice x16, local copies, waits for them, and re-layouts, plane_histogram(): lax.scan(accumulate_plane, jnp.zeros((HISTOGRAM_BINS, HISTOGRAM_BINS), jn...  6 us
    all_to_all x1, starting transfers between devices, trade_parts(): tiles = lax.all_to_all(tiles, axis, split_axis=0, concat_axis=0)  4.84 us
    dot_general x8, matrix products, accumulate_plane(): jnp.dot(dilatation_table, vorticity_table, precision=lax.Precision.HIGHEST)  4.61 us
  transfers between devices with their start and end apart: 7, of which 2 were waited for; matrix products, arithmetic and copies ran while one was open for 11% of the time, Pallas kernels for 0%

profile of v1, /device:TPU:0, one launch (start us, length us, event | category | flops | bytes accessed | tf_op | source)
XLA Modules:
  0.0 204.6 jit_solution(10315833878143292865)
XLA Ops:
  0.7 1.0 pad_maximum_fusion.4
  1.6 1.3 collective-permute-start.1
  2.9 5.5 %collective-permute-start = (f32[5,1,32,32]{3,2,0,1:T(8,128)S(1)}, f32[5,1,32,32]{3,2,0,1:T(8,128)S(1)}, u32[]{:S(2)}, u32[]{:S(2)}) collective-permute-start(f32[5,1,32,32]{3,2,0,1:T(8,128)S(1)} %get-tuple-element.222), channel_id=1, source_target_pairs={{0,2},{2,4},{4,6},{6,8},{8,10},{10,12},{12,14},{14,16},{16,18},{18... | collective-permute-start | bytes 61448 | tf_op jit(solution)/shard_map/ppermute | solution.py:30
  10.2 75.7 %psum.14 = f32[3,32,32]{2,1,0:T(8,128)S(1)} all-reduce(f32[3,32,32]{2,1,0:T(8,128)S(1)} %fusion.50), channel_id=1, replica_groups=mesh['gx'=16,'gy'=2] {'gx'}, use_global_device_ids=true, to_apply=%region_1.2 | all-reduce | flops 3072 | bytes 24576 | tf_op jit(solution)/shard_map/psum | solution.py:160
  88.3 1.3 collective-permute-start.3
  89.6 3.0 %collective-permute-start.2 = (f32[5,10,32,1]{2,3,1,0:T(1,128)S(1)}, f32[5,10,32,1]{2,3,1,0:T(1,128)S(1)}, u32[]{:S(2)}, u32[]{:S(2)}) collective-permute-start(f32[5,10,32,1]{2,3,1,0:T(1,128)S(1)} %copy.81), channel_id=1, source_target_pairs={{0,1},{2,3},{4,5},{6,7},{8,9},{10,11},{12,13},{14,15},{16,17},{18,... | collective-permute-start | bytes 19208 | tf_op jit(solution)/shard_map/ppermute | solution.py:30
  93.3 1.4 and_reduce_fusion
  95.1 1.3 copy.84
  96.3 1.6 pad_maximum_fusion.1
  98.0 1.4 fusion.48
  99.4 1.7 scatter.14
  101.2 1.0 scatter.15
  102.3 0.9 scatter.16
  103.6 3.7 %scatter.19 = f32[5,10,32,34]{3,2,0,1:T(8,128)S(1)} dynamic-update-slice(f32[5,10,32,34]{3,2,0,1:T(8,128)S(1)} %scatter.16, f32[5,8,32,1]{3,2,0,1:T(8,128)S(1)} %slice_select_fusion, s32[]{:T(128)} %constant.328.clone.1, s32[]{:T(128)} %constant.350.clone.1, s32[]{:T(128)} %constant.328.clone.1, s32[]{:T(128)} %constant.351.clone.1) | dynamic-update-slice | bytes 10244 | tf_op jit(solution)/shard_map/scatter | solution.py:172
  109.0 1.2 fusion.90
  110.6 1.0 copy.114
  112.2 3.8 %reduce.27 = f32[1024,8]{1,0:T(8,128)} reduce(f32[1024,1,8]{2,1,0:T(1,128)} %bitcast.192, f32[]{:T(128)} %broadcast.273), dimensions={1}, to_apply=%bitcast.172.reduce_sub_computation | reduce | bytes 65540
  115.9 1.9 reshape.473
  117.9 3.5 %all-to-all-start.1 = ((f32[16,1,512]{2,1,0:T(1,128)}), f32[16,1,512]{2,1,0:T(1,128)S(1)}, u32[]{:S(2)}, u32[]{:S(2)}) async-start(f32[16,1,512]{2,1,0:T(1,128)} %reshape.473), calls=%async_computation.1 | async-start | bytes 65536 | tf_op jit(solution)/shard_map/all_to_all | solution.py:187
  121.4 2.7 %fusion.14 = f32[5,8,32,32]{3,2,0,1:T(8,128)} fusion(f32[5,10,32,34]{3,2,0,1:T(8,128)S(1)} %get-tuple-element.221, f32[5,10,32,34]{3,2,0,1:T(8,128)S(1)} %scatter.19, f32[5,8,1,32]{3,2,0,1:T(1,128)S(1)} %get-tuple-element.213, f32[5,8,31,32]{3,2,0,1:T(8,128)} %get-tuple-element.215, f32[5,8,31,32]{3,2,0,1:T(8,128)S(1)} %get-tuple-element.214, ...), kind=kLoop, calls=%fused_computation.23 | loop fusion | flops 368640 | bytes 4295680 | tf_op jit(solution)/shard_map/sub | solution.py:82
  124.1 1.4 reshape.469
  125.8 0.9 reshape.471
  126.7 2.0 all-to-all-done.1
  128.7 4.8 %all-to-all-start = ((f32[16,1,2560]{2,1,0:T(1,128)}), f32[16,1,2560]{2,1,0:T(1,128)S(1)}, u32[]{:S(2)}, u32[]{:S(2)}) async-start(f32[16,1,2560]{2,1,0:T(1,128)} %reshape.471), calls=%async_computation | async-start | bytes 327680 | tf_op jit(solution)/shard_map/all_to_all | solution.py:19
  135.5 6.0 %all-to-all-done = f32[16,1,2560]{2,1,0:T(1,128)S(1)} async-done(((f32[16,1,2560]{2,1,0:T(1,128)}), f32[16,1,2560]{2,1,0:T(1,128)S(1)}, u32[]{:S(2)}, u32[]{:S(2)}) %all-to-all-start) | async-done | bytes 163872 | tf_op jit(solution)/shard_map/all_to_all | solution.py:19
  141.5 1.0 reduce.26
  143.8 0.9 reshape.475
  144.7 3.5 %all-to-all-start.2 = ((f32[16,1,2560]{2,1,0:T(1,128)}), f32[16,1,2560]{2,1,0:T(1,128)S(1)}, u32[]{:S(2)}, u32[]{:S(2)}) async-start(f32[16,1,2560]{2,1,0:T(1,128)} %reshape.475), calls=%async_computation.2 | async-start | bytes 327680 | tf_op jit(solution)/shard_map/all_to_all | solution.py:191
  148.2 12.6 %while.22 = (s32[]{:T(128)}, f32[64,64]{1,0:T(8,128)S(1)}, s32[8,32,32]{2,1,0:T(8,128)}, s32[8,32,32]{2,1,0:T(8,128)}, f32[8,32,32]{2,1,0:T(8,128)S(1)}, /*index=5*/s32[]{:T(128)}, s32[]{:T(128)}) while((s32[]{:T(128)}, f32[64,64]{1,0:T(8,128)S(1)}, s32[8,32,32]{2,1,0:T(8,128)}, s32[8,32,32]{2,1,0:T(8,128)}, ...), condition=%wide.region_4.5_spmd.clone.clone, body=%wide.region_3.4_spmd.clone.clone.sunk | while | flops 50536448 | bytes 94311 | solution.py:120
  160.8 40.8 %psum.15 = f32[64,64]{1,0:T(8,128)S(1)} all-reduce(f32[64,64]{1,0:T(8,128)S(1)} %get-tuple-element.157), channel_id=1, replica_groups=mesh['gx'=16,'gy'=2] {'gx','gy'}, use_global_device_ids=true, to_apply=%region_5.6 | all-reduce | flops 4096 | bytes 32768 | tf_op jit(solution)/shard_map/psum | solution.py:194
  202.2 1.0 reduce.29
  203.6 1.0 reshape.466
  (144 shorter events, 24.7 us)
Async XLA Ops:
  0.6 142.2 %copy-start = (f32[1,128,128]{2,1,0:T(8,128)S(1)}, f32[1,128,128]{2,1,0:T(8,128)}, u32[]{:S(2)}) copy-start(f32[1,128,128]{2,1,0:T(8,128)} %param.40) | copy-start | bytes 196612
  0.6 85.3 %copy-start.1 = (f32[3,8,32,32]{3,2,1,0:T(8,128)S(1)}, f32[3,8,32,32]{3,2,1,0:T(8,128)}, u32[]{:S(2)}) copy-start(f32[3,8,32,32]{3,2,1,0:T(8,128)} %param.34) | copy-start | bytes 294916
  1.6 85.6 %collective-permute-start.1 = (f32[5,1,32,32]{3,2,0,1:T(8,128)S(1)}, f32[5,1,32,32]{3,2,0,1:T(8,128)S(1)}, u32[]{:S(2)}, u32[]{:S(2)}) collective-permute-start(f32[5,1,32,32]{3,2,0,1:T(8,128)S(1)} %get-tuple-element.223), channel_id=1, source_target_pairs={{2,0},{4,2},{6,4},{8,6},{10,8},{12,10},{14,12},{16,14},{18,16},{20... | collective-permute-start | bytes 61448 | tf_op jit(solution)/shard_map/ppermute | solution.py:31
  2.9 84.3 %collective-permute-start = (f32[5,1,32,32]{3,2,0,1:T(8,128)S(1)}, f32[5,1,32,32]{3,2,0,1:T(8,128)S(1)}, u32[]{:S(2)}, u32[]{:S(2)}) collective-permute-start(f32[5,1,32,32]{3,2,0,1:T(8,128)S(1)} %get-tuple-element.222), channel_id=1, source_target_pairs={{0,2},{2,4},{4,6},{6,8},{8,10},{10,12},{12,14},{14,16},{16,18},{18... | collective-permute-start | bytes 61448 | tf_op jit(solution)/shard_map/ppermute | solution.py:30
  8.4 0.7 copy-start.8
  8.4 0.7 copy-start.7
  9.1 0.7 copy-start.4
  9.1 0.7 copy-start.5
  9.9 76.0 %copy-start.3 = (f32[8,32,32]{2,1,0:T(8,128)S(1)}, f32[8,32,32]{2,1,0:T(8,128)}, u32[]{:S(2)}) copy-start(f32[8,32,32]{2,1,0:T(8,128)} %param.33) | copy-start | bytes 98308
  10.1 75.8 %copy-start.2 = (f32[8,32,32]{2,1,0:T(8,128)S(1)}, f32[8,32,32]{2,1,0:T(8,128)}, u32[]{:S(2)}) copy-start(f32[8,32,32]{2,1,0:T(8,128)} %param.35) | copy-start | bytes 98308
  85.9 0.7 copy-start.9
  88.3 6.7 %collective-permute-start.3 = (f32[5,10,32,1]{2,3,1,0:T(1,128)S(1)}, f32[5,10,32,1]{2,3,1,0:T(1,128)S(1)}, u32[]{:S(2)}, u32[]{:S(2)}) collective-permute-start(f32[5,10,32,1]{2,3,1,0:T(1,128)S(1)} %copy.82), channel_id=1, source_target_pairs={{1,0},{3,2},{5,4},{7,6},{9,8},{11,10},{13,12},{15,14},{17,16},{19,... | collective-permute-start | bytes 19208 | tf_op jit(solution)/shard_map/ppermute | solution.py:31
  89.6 5.1 %collective-permute-start.2 = (f32[5,10,32,1]{2,3,1,0:T(1,128)S(1)}, f32[5,10,32,1]{2,3,1,0:T(1,128)S(1)}, u32[]{:S(2)}, u32[]{:S(2)}) collective-permute-start(f32[5,10,32,1]{2,3,1,0:T(1,128)S(1)} %copy.81), channel_id=1, source_target_pairs={{0,1},{2,3},{4,5},{6,7},{8,9},{10,11},{12,13},{14,15},{16,17},{18,... | collective-permute-start | bytes 19208 | tf_op jit(solution)/shard_map/ppermute | solution.py:30
  92.7 0.7 copy-start.6
  117.9 10.9 %all-to-all-start.1 = ((f32[16,1,512]{2,1,0:T(1,128)}), f32[16,1,512]{2,1,0:T(1,128)S(1)}, u32[]{:S(2)}, u32[]{:S(2)}) async-start(f32[16,1,512]{2,1,0:T(1,128)} %reshape.473), calls=%async_computation.1 | async-start | bytes 65536 | tf_op jit(solution)/shard_map/all_to_all | solution.py:187
  128.7 12.8 %all-to-all-start = ((f32[16,1,2560]{2,1,0:T(1,128)}), f32[16,1,2560]{2,1,0:T(1,128)S(1)}, u32[]{:S(2)}, u32[]{:S(2)}) async-start(f32[16,1,2560]{2,1,0:T(1,128)} %reshape.471), calls=%async_computation | async-start | bytes 327680 | tf_op jit(solution)/shard_map/all_to_all | solution.py:19
  144.7 57.5 %all-to-all-start.2 = ((f32[16,1,2560]{2,1,0:T(1,128)}), f32[16,1,2560]{2,1,0:T(1,128)S(1)}, u32[]{:S(2)}, u32[]{:S(2)}) async-start(f32[16,1,2560]{2,1,0:T(1,128)} %reshape.475), calls=%async_computation.2 | async-start | bytes 327680 | tf_op jit(solution)/shard_map/all_to_all | solution.py:191
